TPU v7x, 32 devices: a whole 2x2x4 slice. The times are simulated.
32 devices in a mesh: ctx: 8 (over y, x, core), tp: 4 (over z).
Axes of the slice: x: 2, y: 2, z: 4, core: 2. Of those that a mesh axis runs over, the one named last changes fastest.
Arguments:
- queries: bfloat16 [2048, 4096], P('ctx', 'tp'), may hold values from -100 to 100
- key_pages: bfloat16 [32, 64, 1024], P('ctx', None, 'tp'), may hold values from -5 to 5
- value_pages: bfloat16 [32, 64, 1024], P('ctx', None, 'tp'), may hold values from -6 to 6
- mixer_input: bfloat16 [2048, 4096], P('ctx', 'tp'), may hold values from -6 to 6
- state_write: bfloat16 [2048, 1024], P('ctx', 'tp'), may hold values from -0.029907227 to 0.029907227
- state_read: bfloat16 [2048, 1024], P('ctx', 'tp'), may hold values from -6 to 6
- log_decay: float32 [32, 2048], P('tp', 'ctx'), may hold values from -1 to 0
- skip_gain: float32 [32], P('tp'), may hold values from 0.5 to 1.5
- doc_lengths: int32 [4], replicated, may hold values from 1 to 1024, 2048 in all
- page_table: int32 [32], replicated, may hold values from 0 to 31, as said below
- attention_weight: bfloat16 [4096, 4096], P('tp'), may hold values from -0.75 to 0.75
- mixer_weight: bfloat16 [4096, 4096], P('tp'), may hold values from -0.09375 to 0.09375
Outputs:
- mixed: bfloat16 [2048, 4096], P(('ctx', 'tp'))
Inputs may be any that keep to these rules, and one draw needn't show every extreme that they name: `doc_lengths`: the lengths sum to 2048; the longest is exactly 1024. `page_table`: A permutation: every physical page holds exactly one logical page.
All inputs are finite; a program needn't handle non-finite values.
Results may differ from a plain program's by a relative error of at most 0.007.
Values may be sent and summed in bfloat16 or wider, within the bound.
No kernel may reach another device: no remote copies, remote signals or barrier semaphores. Data moves between devices by JAX's collectives and lax.ppermute only.
A program may use at most 256 MiB of HBM per device.

v0:
```python
import jax
import jax.numpy as jnp
from jax import lax
from jax.sharding import PartitionSpec as P

HEAD_DIM = 128
SSM_HEAD_DIM = 128
STATE = 128


def entering(array, axis, join, neutral):
    place = lax.axis_index(axis)
    gathered = jax.tree.map(
        lambda a, kind: lax.all_gather(a.astype(kind), axis), array, (jnp.bfloat16, jnp.bfloat16)
    )
    state = jax.tree.map(lambda a, e: jnp.zeros_like(a) + jnp.asarray(e, a.dtype), array, neutral)

    def one(lap, state):
        return join(
            state,
            jax.tree.map(
                lambda a, own: lax.dynamic_index_in_dim(a, lap, 0, False).astype(own.dtype),
                gathered,
                array,
            ),
        )

    return lax.fori_loop(0, place, one, state)


def segment_of(positions, doc_ends):
    return jnp.sum((positions[:, None] >= doc_ends[None, :]).astype(jnp.int32), axis=1)


def mixer_local(head_input, write_rows, read_rows, decay_rows, block_seg, prev_seg, per_group):
    tok_rows = head_input.shape[0]
    decay_sum = jnp.cumsum(decay_rows, axis=1)
    token_order = jnp.arange(tok_rows, dtype=jnp.int32)
    visible = (token_order[None, :] <= token_order[:, None]) & (
        block_seg[None, :] == block_seg[:, None]
    )
    decay_diff = decay_sum[:, :, None] - decay_sum[:, None, :]
    decay_mat = jnp.where(visible[None], jnp.exp(jnp.minimum(decay_diff, 0.0)), 0.0)
    inner_prod = jnp.einsum(
        "tgn,sgn->gts", read_rows, write_rows, preferred_element_type=jnp.float32
    )
    mixing = (decay_mat * jnp.repeat(inner_prod, per_group, axis=0)).astype(jnp.bfloat16)
    intra_out = jnp.einsum("hts,shp->thp", mixing, head_input, preferred_element_type=jnp.float32)
    end_seg = block_seg[-1]
    end_weight = jnp.where(
        (block_seg == end_seg)[None, :], jnp.exp(decay_sum[:, -1:] - decay_sum), 0.0
    )
    write_heads = jnp.repeat(write_rows, per_group, axis=1)
    end_write = (jnp.transpose(end_weight)[:, :, None] * write_heads).astype(jnp.bfloat16)
    block_state = jnp.einsum(
        "thn,thp->hnp", end_write, head_input, preferred_element_type=jnp.float32
    )
    block_gain = jnp.where(end_seg == prev_seg, jnp.exp(decay_sum[:, -1]), 0.0)
    return (intra_out, block_gain, block_state, decay_sum)


def mixer_entry(
    intra_out, decay_sum, read_rows, head_input, skip_gain, block_seg, prev_seg, state_in, per_group
):
    read_heads = jnp.repeat(read_rows, per_group, axis=1).astype(jnp.float32)
    inter_out = jnp.einsum("thn,hnp->thp", read_heads, state_in, precision=lax.Precision.HIGHEST)
    entry_gain = jnp.where((block_seg == prev_seg)[None, :], jnp.exp(decay_sum), 0.0)
    return (
        intra_out
        + jnp.transpose(entry_gain)[:, :, None] * inter_out
        + skip_gain[None, :, None] * head_input.astype(jnp.float32)
    )


def compose_states(earlier, later):
    return (earlier[0] * later[0], later[0][:, None, None] * earlier[1] + later[1])


def shards(
    queries,
    key_pages,
    value_pages,
    mixer_input,
    state_write,
    state_read,
    log_decay,
    skip_gain,
    doc_lengths,
    page_table,
    attention_weight,
    mixer_weight,
):
    my_block = lax.axis_index("ctx")
    tok_rows = queries.shape[0]
    doc_ends = jnp.cumsum(doc_lengths)
    first_pos = my_block * tok_rows
    positions = first_pos + jnp.arange(tok_rows, dtype=jnp.int32)
    query_seg = segment_of(positions, doc_ends)
    head_local = queries.shape[1] // HEAD_DIM
    kv_local = key_pages.shape[2] // HEAD_DIM
    group_size = head_local // kv_local
    page_len = key_pages.shape[1]
    page_total = page_table.shape[0]
    page_ids = jnp.arange(page_total, dtype=jnp.int32)
    logical_of = jnp.sum(
        jnp.where(page_table[:, None] == page_ids[None, :], page_ids[:, None], 0), axis=0
    )
    query_heads = queries.reshape(tok_rows, kv_local, group_size, HEAD_DIM)
    stat_shape = (tok_rows, kv_local, group_size)
    key_rows = lax.all_gather(key_pages, "ctx", axis=0, tiled=True)
    page_count = key_rows.shape[0]
    key_pos = (
        logical_of[:, None] * page_len + jnp.arange(page_len, dtype=jnp.int32)[None, :]
    ).reshape(-1)
    key_seg = segment_of(key_pos, doc_ends)
    visible = (key_pos[None, :] <= positions[:, None]) & (key_seg[None, :] == query_seg[:, None])
    flat_keys = key_rows.reshape(page_count * page_len, kv_local, HEAD_DIM)
    flat_values = lax.all_gather(value_pages, "ctx", axis=0, tiled=True).reshape(
        page_count * page_len, kv_local, HEAD_DIM
    )
    run_max = jnp.full(stat_shape, -1e30, jnp.float32)
    scores = jnp.einsum(
        "tgjd,sgd->tgjs", query_heads, flat_keys, preferred_element_type=jnp.float32
    ) * HEAD_DIM ** (-0.5)
    shown = visible[:, None, None, :]
    new_max = jnp.maximum(run_max, jnp.max(jnp.where(shown, scores, -1e30), axis=3))
    weights = jnp.where(shown, jnp.exp(scores - new_max[..., None]), 0.0)
    new_sum = jnp.sum(weights, axis=3)
    probabilities = weights.astype(jnp.bfloat16)
    new_acc = jnp.einsum(
        "tgjs,sgd->tgjd", probabilities, flat_values, preferred_element_type=jnp.float32
    )
    attention_out = (
        (new_acc / new_sum[..., None]).reshape(tok_rows, head_local * HEAD_DIM).astype(jnp.bfloat16)
    )
    ssm_local = mixer_input.shape[1] // SSM_HEAD_DIM
    group_local = state_write.shape[1] // STATE
    per_group = ssm_local // group_local
    head_input = mixer_input.reshape(tok_rows, ssm_local, SSM_HEAD_DIM)
    write_rows = state_write.reshape(tok_rows, group_local, STATE)
    read_rows = state_read.reshape(tok_rows, group_local, STATE)
    before_pos = jnp.reshape(first_pos - 1, (1,))
    prev_seg = jnp.where(first_pos > 0, segment_of(before_pos, doc_ends)[0], -1)
    intra_out, block_gain, block_state, decay_sum = mixer_local(
        head_input, write_rows, read_rows, log_decay, query_seg, prev_seg, per_group
    )
    gain_in, state_in = entering(
        (block_gain, block_state),
        "ctx",
        compose_states,
        (jnp.ones_like(block_gain), jnp.zeros_like(block_state)),
    )
    mixer_rows = mixer_entry(
        intra_out,
        decay_sum,
        read_rows,
        head_input,
        skip_gain,
        query_seg,
        prev_seg,
        state_in,
        per_group,
    )
    mixer_out = mixer_rows.reshape(tok_rows, ssm_local * SSM_HEAD_DIM).astype(jnp.bfloat16)
    mixed = lax.psum_scatter(
        jnp.dot(attention_out, attention_weight, preferred_element_type=jnp.float32)
        + jnp.dot(mixer_out, mixer_weight, preferred_element_type=jnp.float32),
        "tp",
        scatter_dimension=0,
        tiled=True,
    )
    return mixed.astype(jnp.bfloat16)


def solution(mesh):
    placed = (
        P("ctx", "tp"),
        P("ctx", None, "tp"),
        P("ctx", None, "tp"),
        P("ctx", "tp"),
        P("ctx", "tp"),
        P("ctx", "tp"),
        P("tp", "ctx"),
        P("tp"),
        P(),
        P(),
        P("tp", None),
        P("tp", None),
    )
    return jax.shard_map(
        shards, mesh=mesh, in_specs=placed, out_specs=P(("ctx", "tp"), None), check_vma=False
    )
```

profile of v0, /device:TPU:0, one launch (start us, length us, event | category | flops | bytes accessed | tf_op | source)
XLA Modules:
  0.0 194.3 jit_solution(17334929127929989161)
XLA Ops:
  6.5 0.7 all-gather.6.cloned.1.call-update
  7.3 0.7 all-gather.8.cloned.1.call-update
  8.0 0.0 all-gather.10.cloned.1.call-start
  8.1 0.8 reduce-window.10
  8.9 0.1 convert_reduce_fusion.1
  9.0 0.6 slice.15
  9.6 1.2 reduce-window.11
  10.8 0.2 slice_reduce_fusion
  11.0 1.2 copy.66
  12.3 0.9 reshape.265
  13.2 0.1 copy.67
  13.3 0.6 fusion.30
  14.6 0.7 broadcast_compare_fusion
  15.3 0.1 select_bitcast_fusion.1
  15.3 0.2 slice_reduce_fusion.1
  15.5 0.1 select_bitcast_fusion
  15.6 0.1 fusion.16
  15.7 1.0 convolution_convert_fusion
  16.8 0.0 reduce-scatter.2.cloned.1.call-start
  16.8 0.1 fusion.25
  17.6 1.1 fusion.26
  18.7 0.7 select_reduce_fusion
  19.5 0.1 iota_add_fusion
  19.6 0.1 add.64
  19.6 0.1 convert_reduce_fusion
  19.7 1.4 compare_and_fusion
  21.2 2.2 %reshape.260 = bf16[256,2,4,128]{3,2,1,0:T(4,128)(2,1)} reshape(bf16[256,1024]{1,0:T(8,128)(2,1)} %param.14) | data formatting | bytes 1048576 | tf_op jit(solution)/shard_map/reshape | solution.py:108
  23.4 0.5 fusion.8
  23.9 0.5 convolution_bitcast_fusion.1
  24.4 0.2 fusion.29
  24.6 0.7 dynamic-slice
  26.0 0.2 dynamic-update-slice
  26.2 15.3 %all-reduce = bf16[64]{0:T(256)(128)(2,1)S(1)} all-reduce(bf16[64]{0:T(256)(128)(2,1)S(1)} %dynamic-update-slice), channel_id=2, replica_groups=mesh['ctx'=8,'tp'=4] {'ctx'}, use_global_device_ids=true, to_apply=%add | all-reduce | flops 64 | bytes 256
  41.6 0.1 reshape.271
  41.7 1.3 reshape.259
  43.0 8.3 %fusion = (f32[256,2,4]{0,2,1:T(4,128)S(1)}, f32[2,2048,256,4]{2,1,3,0:T(8,128)}) fusion(pred[256,2048]{0,1:T(8,128)(4,1)S(1)} %compare_and_fusion, bf16[256,2,4,128]{3,2,1,0:T(4,128)(2,1)} %reshape.260, bf16[2048,2,128,1]{2,1,0,3:T(2,128)(2,1)S(1)} %bitcast.103), kind=kOutput, calls=%fused_computation.4 | convolution fusion | flops 1086322688 | bytes 18882560 | tf_op jit(solution)/shard_map/tgjd,sgd->tgjs/dot_general | solution.py:122
  51.3 9.7 %all-gather.8.cloned.1.call-done = bf16[32,64,256]{2,1,0:T(8,128)(2,1)} async-done(((bf16[4,64,256]{2,1,0:T(8,128)(2,1)}), bf16[32,64,256]{2,1,0:T(8,128)(2,1)}) %all-gather.8.cloned.1.call-update) | async-done | bytes 1048592 | tf_op jit(solution)/shard_map/all_gather | solution.py:118
  61.0 1.3 reshape.261
  62.4 9.2 %fusion.3 = f32[256,2,4]{0,2,1:T(4,128)S(1)} fusion(f32[2,2048,256,4]{2,1,3,0:T(8,128)} %get-tuple-element.65, f32[256,2,4]{0,2,1:T(4,128)S(1)} %broadcast_maximum_fusion, pred[256,2048]{0,1:T(8,128)(4,1)S(1)} %compare_and_fusion), kind=kLoop, calls=%fused_computation.7 | loop fusion | flops 16775168 | bytes 17317888 | tf_op jit(solution)/shard_map/reduce_sum | solution.py:128
  71.5 7.8 %divide_convert_fusion = bf16[256,2,4,128]{0,3,2,1:T(8,128)(2,1)S(1)} fusion(f32[2,2048,256,4]{2,1,3,0:T(8,128)} %get-tuple-element.65, f32[256,2,4]{0,2,1:T(4,128)S(1)} %broadcast_maximum_fusion, pred[256,2048]{0,1:T(8,128)(4,1)S(1)} %compare_and_fusion, bf16[2048,2,128,1]{2,1,0,3:T(2,128)(2,1)S(1)} %bitcast.102, f32[256,2,4]{0,2,1:T(4,128)S(1)} %fusion.3), kind=kOutput, calls=%fused_computation.28 | convolution fusion | flops 1091043328 | bytes 18890752 | tf_op jit(solution)/shard_map/tgjs,sgd->tgjd/dot_general | solution.py:130
  79.3 8.0 %fusion.33 = f32[256,4096]{1,0:T(8,128)} fusion(bf16[256,1024]{0,1:T(8,128)(2,1)S(1)} %bitcast.105, bf16[1024,4096]{1,0:T(8,128)(2,1)} %param.24), kind=kOutput, calls=%fused_computation.57 | convolution fusion | flops 2147483648 | bytes 13107200 | tf_op jit(solution)/shard_map/dot_general | solution.py:166
  87.4 3.4 %all-gather.10.cloned.1.call-done = bf16[64,128,128]{2,1,0:T(8,128)(2,1)} async-done(((bf16[8,128,128]{2,1,0:T(8,128)(2,1)}), bf16[64,128,128]{2,1,0:T(8,128)(2,1)}) %all-gather.10.cloned.1.call-update) | async-done | bytes 2097168 | tf_op jit(solution)/shard_map/all_gather | solution.py:14
  90.9 0.2 while.12
  91.1 0.1 broadcast_in_dim.120
  91.2 0.7 fusion.15
  91.9 8.9 %convolution_add_fusion = f32[256,4096]{1,0:T(8,128)} fusion(f32[256,4096]{1,0:T(8,128)} %fusion.33, bf16[256,1024]{0,1:T(8,128)(2,1)S(1)} %bitcast.101, bf16[1024,4096]{1,0:T(8,128)(2,1)} %param.25), kind=kOutput, calls=%fused_computation.11 | convolution fusion | flops 2148532224 | bytes 17301504 | tf_op jit(solution)/shard_map/dot_general | solution.py:167
  100.9 84.8 %reduce-scatter.2.cloned.1.call-done = f32[64,4096]{1,0:T(8,128)} async-done(((f32[256,4096]{1,0:T(8,128)}), f32[64,4096]{1,0:T(8,128)}) %reduce-scatter.2.cloned.1.call-update) | async-done | bytes 1048592 | tf_op jit(solution)/shard_map/reduce_scatter | solution.py:165
  185.7 2.1 %convert_element_type.103 = bf16[64,4096]{1,0:T(8,128)(2,1)} convert(f32[64,4096]{1,0:T(8,128)} %reduce-scatter.2.cloned.1.call-done) | non-fusion elementwise | flops 262144 | bytes 1572864 | tf_op jit(solution)/shard_map/convert_element_type | solution.py:172
  (19 shorter events, 0.2 us)
Async XLA Ops:
  6.5 11.0 %copy-start = (bf16[256,256]{1,0:T(8,128)(2,1)S(1)}, bf16[256,256]{1,0:T(8,128)(2,1)}, u32[]{:S(2)}) copy-start(bf16[256,256]{1,0:T(8,128)(2,1)} %param.19) | copy-start | bytes 393220
  6.5 18.1 %copy-start.2 = (u32[32]{0:T(128)S(1)}, u32[32]{0:T(128)}, u32[]{:S(2)}) copy-start(u32[32]{0:T(128)} %constant.53) | copy-start | bytes 388
  6.5 35.1 %all-gather.6.cloned.1.call-start = ((), (), s32[]{:S(2)}) async-start(), calls=%async_computation.1 | async-start | bytes 1179648 | tf_op jit(solution)/shard_map/all_gather | solution.py:110
  7.3 53.7 %all-gather.8.cloned.1.call-start = ((), (), s32[]{:S(2)}) async-start(), calls=%async_computation.2 | async-start | bytes 1179648 | tf_op jit(solution)/shard_map/all_gather | solution.py:118
  8.0 82.8 %all-gather.10.cloned.1.call-start = ((), (), s32[]{:S(2)}) async-start(), calls=%async_computation.4 | async-start | bytes 2359296 | tf_op jit(solution)/shard_map/all_gather | solution.py:14
  16.8 169.0 %reduce-scatter.2.cloned.1.call-start = ((), (), s32[]{:S(2)}) async-start(), calls=%async_computation.3 | async-start | bytes 5242880 | tf_op jit(solution)/shard_map/reduce_scatter | solution.py:165
  79.3 11.8 %copy-start.1 = (f32[8]{0:T(128)S(1)}, f32[8]{0:T(128)}, u32[]{:S(2)}) copy-start(f32[8]{0:T(128)} %param.21) | copy-start | bytes 100
Sparse Core Ops, SparseCore 0:
  9.2 26.3 all-gather.5
  37.5 23.4 all-gather.7
  62.9 27.8 all-gather.9
  101.0 84.6 reduce-scatter.1
where the time goes:
time: 195 us; the launch traced here: 194 us
  waiting for transfers between devices  99.4 us (51%)
  matrix products  36.4 us (19%)
  other arithmetic  18.2 us (9%)
  blocking collectives  15.3 us (8%)
  between operations  15.3 us (8%)
  local copies, waits for them, and re-layouts  9.32 us (5%)
    reduce_scatter x1, waiting for transfers between devices, shards(): lax.psum_scatter(jnp.dot(attention_out, attention_weight, preferred_eleme...  84.8 us
    unnamed x1, blocking collectives  15.3 us
    all_gather x1, waiting for transfers between devices, shards(): lax.all_gather(value_pages, 'ctx', axis=0, tiled=True)  9.7 us
    reduce_sum x1, other arithmetic, shards(): new_sum = jnp.sum(weights, axis=3)  9.17 us
    dot_general x1, matrix products, shards(): jnp.dot(mixer_out, mixer_weight, preferred_element_type=jnp.float32)  8.91 us
    dot_general x1, matrix products, shards(): jnp.einsum('tgjd,sgd->tgjs', query_heads, flat_keys, preferred_element_ty...  8.3 us
    dot_general x1, matrix products, shards(): jnp.dot(attention_out, attention_weight, preferred_element_type=jnp.float32)  8.04 us
    dot_general x1, matrix products, shards(): jnp.einsum('tgjs,sgd->tgjd', probabilities, flat_values, preferred_elemen...  7.79 us
  transfers between devices with their start and end apart: 4, of which 3 were waited for; matrix products, arithmetic and copies ran while one was open for 27% of the time, Pallas kernels for 0%

commit v1 on v0

--- a/solution.py
+++ b/solution.py
@@ -6,6 +6,22 @@
 HEAD_DIM = 128
 SSM_HEAD_DIM = 128
 STATE = 128
+
+
+def collect(x, axis, dim):
+    ways, here, step = (lax.axis_size(axis), lax.axis_index(axis), x.shape[dim])
+    shape = [n * ways if d == dim else n for d, n in enumerate(x.shape)]
+    full = lax.dynamic_update_slice_in_dim(jnp.zeros(shape, x.dtype), x, here * step, axis=dim)
+    going_up = going_down = x
+    for far in range(1, ways // 2 + 1):
+        going_up = lax.ppermute(going_up, axis, [(d, (d + 1) % ways) for d in range(ways)])
+        full = lax.dynamic_update_slice_in_dim(full, going_up, (here - far) % ways * step, axis=dim)
+        if 2 * far < ways:
+            going_down = lax.ppermute(going_down, axis, [(d, (d - 1) % ways) for d in range(ways)])
+            full = lax.dynamic_update_slice_in_dim(
+                full, going_down, (here + far) % ways * step, axis=dim
+            )
+    return full
 
 
 def entering(array, axis, join, neutral):
@@ -115,9 +131,7 @@
     key_seg = segment_of(key_pos, doc_ends)
     visible = (key_pos[None, :] <= positions[:, None]) & (key_seg[None, :] == query_seg[:, None])
     flat_keys = key_rows.reshape(page_count * page_len, kv_local, HEAD_DIM)
-    flat_values = lax.all_gather(value_pages, "ctx", axis=0, tiled=True).reshape(
-        page_count * page_len, kv_local, HEAD_DIM
-    )
+    flat_values = collect(value_pages, "ctx", 0).reshape(page_count * page_len, kv_local, HEAD_DIM)
     run_max = jnp.full(stat_shape, -1e30, jnp.float32)
     scores = jnp.einsum(
         "tgjd,sgd->tgjs", query_heads, flat_keys, preferred_element_type=jnp.float32

time: 195 us -> 197 us (1.010)
  starting transfers between devices: 0.12 us -> 9 us
  waiting for transfers between devices: 99.4 us -> 95 us
  blocking collectives: 15.3 us -> 12.6 us
    ppermute x0 -> x7, waiting for transfers between devices: none -> 11.3 us  [the longest x4 8.3 us: collect(): lax.ppermute(going_up, axis, [(d, (d + 1) % ways) for d in range(ways)])]
    all_gather x1 -> x0, waiting for transfers between devices: 9.7 us -> none  [shards(): lax.all_gather(value_pages, 'ctx', axis=0, tiled=True)]
    ppermute x0 -> x7, starting transfers between devices: none -> 8.89 us  [the longest x3 8.32 us: collect(): lax.ppermute(going_down, axis, [(d, (d - 1) % ways) for d in range(ways)])]
    all_gather x1, waiting for transfers between devices: 3.44 us -> 0.01 us  [entering(): lax.all_gather(a.astype(kind), axis)]
    unnamed x1, blocking collectives: 15.3 us -> 12.6 us
  transfers between devices with their start and end apart: 4 -> 10, of which waited for: 3 -> 6; matrix products, arithmetic and copies ran while one was open for 27% -> 27% of each run, Pallas kernels for 0% -> 0%
where the time goes in v1:
time: 197 us
  waiting for transfers between devices  95 us (48%)
  matrix products  36 us (18%)
  other arithmetic  18.3 us (9%)
  between operations  15.4 us (8%)
  blocking collectives  12.6 us (6%)
  local copies, waits for them, and re-layouts  10 us (5%)
  starting transfers between devices  9 us (5%)
    reduce_scatter x1, waiting for transfers between devices, shards(): lax.psum_scatter(jnp.dot(attention_out, attention_weight, preferred_eleme...  83 us
    unnamed x1, blocking collectives  12.6 us
    reduce_sum x1, other arithmetic, shards(): new_sum = jnp.sum(weights, axis=3)  9.25 us
    dot_general x1, matrix products, shards(): jnp.dot(mixer_out, mixer_weight, preferred_element_type=jnp.float32)  8.91 us
    dot_general x1, matrix products, shards(): jnp.einsum('tgjd,sgd->tgjs', query_heads, flat_keys, preferred_element_ty...  8.33 us
    ppermute x3, starting transfers between devices, collect(): lax.ppermute(going_down, axis, [(d, (d - 1) % ways) for d in range(ways)])  8.32 us
    ppermute x4, waiting for transfers between devices, collect(): lax.ppermute(going_up, axis, [(d, (d + 1) % ways) for d in range(ways)])  8.3 us
    dot_general x1, matrix products, shards(): jnp.dot(attention_out, attention_weight, preferred_element_type=jnp.float32)  7.69 us
  transfers between devices with their start and end apart: 10, of which 6 were waited for; matrix products, arithmetic and copies ran while one was open for 27% of the time, Pallas kernels for 0%

profile of v1, /device:TPU:0, one launch (start us, length us, event | category | flops | bytes accessed | tf_op | source)
XLA Modules:
  0.0 196.5 jit_solution(11498557902759186614)
XLA Ops:
  6.6 0.7 all-gather.5.cloned.1.call-update
  7.3 0.5 collective-permute-start
  7.8 2.9 %collective-permute-start.1 = (bf16[4,64,256]{2,1,0:T(8,128)(2,1)}, bf16[4,64,256]{2,1,0:T(8,128)(2,1)}, u32[]{:S(2)}, u32[]{:S(2)}) collective-permute-start(bf16[4,64,256]{2,1,0:T(8,128)(2,1)} %param.16), channel_id=1, source_target_pairs={{0,28},{4,0},{8,4},{12,8},{16,12},{20,16},{24,20},{28,24},{1,29},{... | collective-permute-start | bytes 393224 | tf_op jit(solution)/shard_map/ppermute | solution.py:20
  10.8 0.8 reduce-window.10
  11.7 0.6 slice.15
  12.3 1.2 reduce-window.11
  13.5 0.2 slice_reduce_fusion
  13.7 1.2 copy.73
  15.0 0.9 reshape.265
  15.9 0.1 copy.74
  16.0 0.6 fusion.30
  17.3 0.7 broadcast_compare_fusion
  18.0 0.2 slice_reduce_fusion.1
  18.3 0.1 fusion.16
  18.4 1.0 convolution_convert_fusion
  19.5 0.1 fusion.25
  20.3 1.1 fusion.26
  21.5 0.7 select_reduce_fusion
  22.4 0.1 convert_reduce_fusion
  22.5 1.4 compare_and_fusion
  23.9 0.5 fusion.8
  24.4 0.5 convolution_bitcast_fusion.1
  24.9 0.2 fusion.29
  25.2 1.2 reshape.261
  26.4 0.6 dynamic-slice
  27.6 0.2 dynamic-update-slice
  27.9 12.6 %all-reduce = bf16[64]{0:T(256)(128)(2,1)S(1)} all-reduce(bf16[64]{0:T(256)(128)(2,1)S(1)} %dynamic-update-slice), channel_id=2, replica_groups=mesh['ctx'=8,'tp'=4] {'ctx'}, use_global_device_ids=true, to_apply=%add | all-reduce | flops 64 | bytes 256
  40.6 0.1 broadcast_in_dim.109
  40.8 2.6 %collective-permute-start.3 = (bf16[4,64,256]{2,1,0:T(8,128)(2,1)}, bf16[4,64,256]{2,1,0:T(8,128)(2,1)S(1)}, u32[]{:S(2)}, u32[]{:S(2)}) collective-permute-start(bf16[4,64,256]{2,1,0:T(8,128)(2,1)} %collective-permute-done.1), channel_id=1, source_target_pairs={{0,28},{4,0},{8,4},{12,8},{16,12},{20,16},{24,20},{28,24},{1,29},{... | collective-permute-start | bytes 393224 | tf_op jit(solution)/shard_map/ppermute | solution.py:20
  43.4 0.9 constant_dynamic-update-slice_fusion.6
  44.4 0.9 constant_dynamic-update-slice_fusion.5
  45.3 2.3 %collective-permute-done.2 = bf16[4,64,256]{2,1,0:T(8,128)(2,1)S(1)} collective-permute-done((bf16[4,64,256]{2,1,0:T(8,128)(2,1)}, bf16[4,64,256]{2,1,0:T(8,128)(2,1)S(1)}, u32[]{:S(2)}, u32[]{:S(2)}) %collective-permute-start.2) | collective-permute-done | bytes 131104 | tf_op jit(solution)/shard_map/ppermute | solution.py:17
  47.6 1.5 collective-permute-done.3
  49.1 2.7 %collective-permute-start.5 = (bf16[4,64,256]{2,1,0:T(8,128)(2,1)S(1)}, bf16[4,64,256]{2,1,0:T(8,128)(2,1)S(1)}, u32[]{:S(2)}, u32[]{:S(2)}) collective-permute-start(bf16[4,64,256]{2,1,0:T(8,128)(2,1)S(1)} %collective-permute-done.3), channel_id=1, source_target_pairs={{0,28},{4,0},{8,4},{12,8},{16,12},{20,16},{24,20},{28,24},{1,29},{... | collective-permute-start | bytes 393224 | tf_op jit(solution)/shard_map/ppermute | solution.py:20
  51.9 2.2 %collective-permute-done.4 = bf16[4,64,256]{2,1,0:T(8,128)(2,1)S(1)} collective-permute-done((bf16[4,64,256]{2,1,0:T(8,128)(2,1)S(1)}, bf16[4,64,256]{2,1,0:T(8,128)(2,1)S(1)}, u32[]{:S(2)}, u32[]{:S(2)}) %collective-permute-start.4) | collective-permute-done | bytes 131104 | tf_op jit(solution)/shard_map/ppermute | solution.py:17
  54.1 1.4 collective-permute-done.5
  55.6 3.8 %collective-permute-done.6 = bf16[4,64,256]{2,1,0:T(8,128)(2,1)S(1)} collective-permute-done((bf16[4,64,256]{2,1,0:T(8,128)(2,1)S(1)}, bf16[4,64,256]{2,1,0:T(8,128)(2,1)S(1)}, u32[]{:S(2)}, u32[]{:S(2)}) %collective-permute-start.6) | collective-permute-done | bytes 131104 | tf_op jit(solution)/shard_map/ppermute | solution.py:17
  59.4 1.1 reshape.258
  60.5 1.3 reshape.260
  61.9 8.3 %fusion = (f32[256,2,4]{0,2,1:T(4,128)S(1)}, f32[2,2048,256,4]{2,1,3,0:T(8,128)}) fusion(pred[256,2048]{0,1:T(8,128)(4,1)S(1)} %compare_and_fusion, bf16[256,2,4,128]{3,2,1,0:T(4,128)(2,1)} %reshape.261, bf16[2048,2,128,1]{2,1,0,3:T(2,128)(2,1)S(1)} %bitcast.103), kind=kOutput, calls=%fused_computation.4 | convolution fusion | flops 1086322688 | bytes 18882560 | tf_op jit(solution)/shard_map/tgjd,sgd->tgjs/dot_general | solution.py:136
  70.2 9.3 %fusion.3 = f32[256,2,4]{0,2,1:T(4,128)S(1)} fusion(f32[2,2048,256,4]{2,1,3,0:T(8,128)} %get-tuple-element.65, f32[256,2,4]{0,2,1:T(4,128)S(1)} %broadcast_maximum_fusion, pred[256,2048]{0,1:T(8,128)(4,1)S(1)} %compare_and_fusion), kind=kLoop, calls=%fused_computation.7 | loop fusion | flops 16775168 | bytes 17317888 | tf_op jit(solution)/shard_map/reduce_sum | solution.py:142
  79.5 7.7 %divide_convert_fusion = bf16[256,2,4,128]{0,3,2,1:T(8,128)(2,1)S(1)} fusion(f32[2,2048,256,4]{2,1,3,0:T(8,128)} %get-tuple-element.65, f32[256,2,4]{0,2,1:T(4,128)S(1)} %broadcast_maximum_fusion, pred[256,2048]{0,1:T(8,128)(4,1)S(1)} %compare_and_fusion, bf16[2048,2,128,1]{2,1,0,3:T(2,128)(2,1)S(1)} %bitcast.102, f32[256,2,4]{0,2,1:T(4,128)S(1)} %fusion.3), kind=kOutput, calls=%fused_computation.28 | convolution fusion | flops 1091043328 | bytes 18890752 | tf_op jit(solution)/shard_map/tgjs,sgd->tgjd/dot_general | solution.py:144
  87.2 7.7 %fusion.33 = f32[256,4096]{1,0:T(8,128)} fusion(bf16[256,1024]{0,1:T(8,128)(2,1)S(1)} %bitcast.105, bf16[1024,4096]{1,0:T(8,128)(2,1)} %param.24), kind=kOutput, calls=%fused_computation.65 | convolution fusion | flops 2147483648 | bytes 13107200 | tf_op jit(solution)/shard_map/dot_general | solution.py:180
  94.9 0.2 while.12
  95.2 0.7 fusion.15
  96.0 8.9 %convolution_add_fusion = f32[256,4096]{1,0:T(8,128)} fusion(f32[256,4096]{1,0:T(8,128)} %fusion.33, bf16[256,1024]{0,1:T(8,128)(2,1)S(1)} %bitcast.101, bf16[1024,4096]{1,0:T(8,128)(2,1)} %param.25), kind=kOutput, calls=%fused_computation.11 | convolution fusion | flops 2148532224 | bytes 17301504 | tf_op jit(solution)/shard_map/dot_general | solution.py:181
  104.9 83.0 %reduce-scatter.2.cloned.1.call-done = f32[64,4096]{1,0:T(8,128)} async-done(((f32[256,4096]{1,0:T(8,128)}), f32[64,4096]{1,0:T(8,128)}) %reduce-scatter.2.cloned.1.call-update) | async-done | bytes 1048592 | tf_op jit(solution)/shard_map/reduce_scatter | solution.py:179
  187.9 2.1 %convert_element_type.103 = bf16[64,4096]{1,0:T(8,128)(2,1)} convert(f32[64,4096]{1,0:T(8,128)} %reduce-scatter.2.cloned.1.call-done) | non-fusion elementwise | flops 262144 | bytes 1572864 | tf_op jit(solution)/shard_map/convert_element_type | solution.py:186
  (45 shorter events, 1.0 us)
Async XLA Ops:
  6.5 13.8 %copy-start = (bf16[256,256]{1,0:T(8,128)(2,1)S(1)}, bf16[256,256]{1,0:T(8,128)(2,1)}, u32[]{:S(2)}) copy-start(bf16[256,256]{1,0:T(8,128)(2,1)} %param.19) | copy-start | bytes 393220
  6.5 19.9 %copy-start.5 = (u32[32]{0:T(128)S(1)}, u32[32]{0:T(128)}, u32[]{:S(2)}) copy-start(u32[32]{0:T(128)} %constant.107) | copy-start | bytes 388
  6.5 34.2 %copy-start.3 = (bf16[4,64,256]{2,1,0:T(8,128)(2,1)S(1)}, bf16[4,64,256]{2,1,0:T(8,128)(2,1)}, u32[]{:S(2)}) copy-start(bf16[4,64,256]{2,1,0:T(8,128)(2,1)} %param.16) | copy-start | bytes 393220
  6.5 18.7 %copy-start.2 = (bf16[256,1024]{1,0:T(8,128)(2,1)S(1)}, bf16[256,1024]{1,0:T(8,128)(2,1)}, u32[]{:S(2)}) copy-start(bf16[256,1024]{1,0:T(8,128)(2,1)} %param.14) | copy-start | bytes 1572868
  6.5 54.0 %all-gather.5.cloned.1.call-start = ((), (), s32[]{:S(2)}) async-start(), calls=%async_computation.1 | async-start | bytes 1179648 | tf_op jit(solution)/shard_map/all_gather | solution.py:126
  7.3 87.6 %all-gather.7.cloned.1.call-start = ((), (), s32[]{:S(2)}) async-start(), calls=%async_computation.3 | async-start | bytes 2359296 | tf_op jit(solution)/shard_map/all_gather | solution.py:30
  7.3 33.4 %collective-permute-start = (bf16[4,64,256]{2,1,0:T(8,128)(2,1)}, bf16[4,64,256]{2,1,0:T(8,128)(2,1)}, u32[]{:S(2)}, u32[]{:S(2)}) collective-permute-start(bf16[4,64,256]{2,1,0:T(8,128)(2,1)} %param.16), channel_id=1, source_target_pairs={{0,4},{4,8},{8,12},{12,16},{16,20},{20,24},{24,28},{28,0},{1,5},{5... | collective-permute-start | bytes 393224 | tf_op jit(solution)/shard_map/ppermute | solution.py:17
  7.8 33.0 %collective-permute-start.1 = (bf16[4,64,256]{2,1,0:T(8,128)(2,1)}, bf16[4,64,256]{2,1,0:T(8,128)(2,1)}, u32[]{:S(2)}, u32[]{:S(2)}) collective-permute-start(bf16[4,64,256]{2,1,0:T(8,128)(2,1)} %param.16), channel_id=1, source_target_pairs={{0,28},{4,0},{8,4},{12,8},{16,12},{20,16},{24,20},{28,24},{1,29},{... | collective-permute-start | bytes 393224 | tf_op jit(solution)/shard_map/ppermute | solution.py:20
  19.5 168.5 %reduce-scatter.2.cloned.1.call-start = ((), (), s32[]{:S(2)}) async-start(), calls=%async_computation.2 | async-start | bytes 5242880 | tf_op jit(solution)/shard_map/reduce_scatter | solution.py:179
  40.7 6.9 %collective-permute-start.2 = (bf16[4,64,256]{2,1,0:T(8,128)(2,1)}, bf16[4,64,256]{2,1,0:T(8,128)(2,1)S(1)}, u32[]{:S(2)}, u32[]{:S(2)}) collective-permute-start(bf16[4,64,256]{2,1,0:T(8,128)(2,1)} %collective-permute-done), channel_id=1, source_target_pairs={{0,4},{4,8},{8,12},{12,16},{16,20},{20,24},{24,28},{28,0},{1,5},{5... | collective-permute-start | bytes 393224 | tf_op jit(solution)/shard_map/ppermute | solution.py:17
  40.8 8.3 %collective-permute-start.3 = (bf16[4,64,256]{2,1,0:T(8,128)(2,1)}, bf16[4,64,256]{2,1,0:T(8,128)(2,1)S(1)}, u32[]{:S(2)}, u32[]{:S(2)}) collective-permute-start(bf16[4,64,256]{2,1,0:T(8,128)(2,1)} %collective-permute-done.1), channel_id=1, source_target_pairs={{0,28},{4,0},{8,4},{12,8},{16,12},{20,16},{24,20},{28,24},{1,29},{... | collective-permute-start | bytes 393224 | tf_op jit(solution)/shard_map/ppermute | solution.py:20
  47.6 6.5 %collective-permute-start.4 = (bf16[4,64,256]{2,1,0:T(8,128)(2,1)S(1)}, bf16[4,64,256]{2,1,0:T(8,128)(2,1)S(1)}, u32[]{:S(2)}, u32[]{:S(2)}) collective-permute-start(bf16[4,64,256]{2,1,0:T(8,128)(2,1)S(1)} %collective-permute-done.2), channel_id=1, source_target_pairs={{0,4},{4,8},{8,12},{12,16},{16,20},{20,24},{24,28},{28,0},{1,5},{5... | collective-permute-start | bytes 393224 | tf_op jit(solution)/shard_map/ppermute | solution.py:17
  49.1 6.4 %collective-permute-start.5 = (bf16[4,64,256]{2,1,0:T(8,128)(2,1)S(1)}, bf16[4,64,256]{2,1,0:T(8,128)(2,1)S(1)}, u32[]{:S(2)}, u32[]{:S(2)}) collective-permute-start(bf16[4,64,256]{2,1,0:T(8,128)(2,1)S(1)} %collective-permute-done.3), channel_id=1, source_target_pairs={{0,28},{4,0},{8,4},{12,8},{16,12},{20,16},{24,20},{28,24},{1,29},{... | collective-permute-start | bytes 393224 | tf_op jit(solution)/shard_map/ppermute | solution.py:20
  54.1 5.3 %collective-permute-start.6 = (bf16[4,64,256]{2,1,0:T(8,128)(2,1)S(1)}, bf16[4,64,256]{2,1,0:T(8,128)(2,1)S(1)}, u32[]{:S(2)}, u32[]{:S(2)}) collective-permute-start(bf16[4,64,256]{2,1,0:T(8,128)(2,1)S(1)} %collective-permute-done.4), channel_id=1, source_target_pairs={{0,4},{4,8},{8,12},{12,16},{16,20},{20,24},{24,28},{28,0},{1,5},{5... | collective-permute-start | bytes 393224 | tf_op jit(solution)/shard_map/ppermute | solution.py:17
  70.2 9.3 %copy-start.1 = (bf16[2048,2,128]{2,1,0:T(2,128)(2,1)S(1)}, bf16[2048,2,128]{2,1,0:T(2,128)(2,1)}, u32[]{:S(2)}) copy-start(bf16[2048,2,128]{2,1,0:T(2,128)(2,1)} %reshape.258) | copy-start | bytes 3145732
  87.2 8.1 %copy-start.4 = (f32[8]{0:T(128)S(1)}, f32[8]{0:T(128)}, u32[]{:S(2)}) copy-start(f32[8]{0:T(128)} %param.21) | copy-start | bytes 100
Sparse Core Ops, SparseCore 0:
  9.3 26.2 all-gather.4
  37.5 30.0 all-gather.6
  105.0 82.8 reduce-scatter.1
